TPU v7x, 32 devices: a whole 2x2x4 slice. The times are simulated.
32 devices in a mesh: groups: 2 (over x), sensor: 16 (over z, y, core).
Axes of the slice: x: 2, y: 2, z: 4, core: 2. Of those that a mesh axis runs over, the one named last changes fastest.
Arguments:
- series: float32 [288, 1536], P(None, ('groups', 'sensor')), parts along dimension 1, may hold values from -6 to 6
- starts: int32 [2], P('groups'), parts along dimension 0, may hold values from 0 to 276
- sensor_order: int32 [1536], P(('groups', 'sensor')), parts along dimension 0, may hold values from 0 to 767, each once
- emb_src: float32 [10, 1536], P(None, ('groups', 'sensor')), parts along dimension 1, may hold values from -4.4 to 330
- emb_dst: float32 [10, 1536], P(None, ('groups', 'sensor')), parts along dimension 1, may hold values from -4.4 to 4.4
- start_proj: float32 [2, 32], replicated, may hold values from -4 to 4
- conv_weight: bfloat16 [64, 64], replicated, may hold values from -0.75 to 0.75
- mix_weight: bfloat16 [96, 32], replicated, may hold values from -0.625 to 0.625
- out_grad: bfloat16 [1536, 384], P(('groups', 'sensor')), parts along dimension 0, may hold values from -0.59765625 to 0.59765625
Outputs:
- layer_out: bfloat16 [1536, 384], P(('groups', 'sensor')), parts along dimension 0
- grad_src: float32 [10, 1536], P(None, ('groups', 'sensor')), parts along dimension 1
- grad_dst: float32 [10, 1536], P(None, ('groups', 'sensor')), parts along dimension 1
- grad_mix: float32 [192, 32], P('groups'), parts along dimension 0
There are 2 independent parts, one for each index of `groups`. A program takes and returns all parts, laid end to end along the dimension named above; an argument that names none is the same for every part. Nothing has to cross between parts.
All inputs are finite; a program needn't handle non-finite values.
Results may differ from a plain program's by a relative error of at most 0.035.
Values may be sent and summed in bfloat16 or wider, within the bound.
A program may use at most 64 MiB of HBM per device.

v0:
```python
import math

import jax
import jax.numpy as jnp
from jax import lax
from jax.sharding import PartitionSpec as P

STEPS = 12


highest = lax.Precision.HIGHEST


def front(readings, start_proj, conv_weight):
    sensors_here = readings.shape[0]
    channels = start_proj.shape[1]
    padded = jnp.concatenate(
        [jnp.zeros(readings.shape[:-1] + (1,), jnp.float32), readings], axis=-1
    )
    inputs = (padded[..., None] * start_proj[0] + start_proj[1]).astype(jnp.bfloat16)
    paired = jnp.concatenate([inputs[:, :, :-1, :], inputs[:, :, 1:, :]], axis=-1).reshape(
        -1, 2 * channels
    )
    gate_terms = jnp.dot(paired, conv_weight, preferred_element_type=jnp.float32)
    hidden = (jnp.tanh(gate_terms[:, :channels]) * jax.nn.sigmoid(gate_terms[:, channels:])).astype(
        jnp.bfloat16
    )
    return (hidden.reshape(sensors_here, -1), inputs[:, :, 1:, :].reshape(sensors_here, -1))


def mixing(residual, hidden, diffused, second, mix_weight):
    channels = mix_weight.shape[1]
    stacked = jnp.concatenate(
        [member.reshape(-1, channels) for member in (hidden, diffused, second)], axis=1
    )
    summed = residual.reshape(-1, channels).astype(jnp.float32) + jnp.dot(
        stacked, mix_weight, preferred_element_type=jnp.float32
    )
    return (summed.astype(jnp.bfloat16).reshape(hidden.shape[0], -1), stacked)


def channel_grads(out_grad, mix_weight):
    channels = mix_weight.shape[1]
    row_count = out_grad.shape[0]
    flat_grad = out_grad.reshape(-1, channels)
    dims = (((1,), (1,)), ((), ()))
    grad_once = lax.dot_general(
        flat_grad, mix_weight[channels : 2 * channels], dims, preferred_element_type=jnp.float32
    )
    grad_twice = lax.dot_general(
        flat_grad, mix_weight[2 * channels :], dims, preferred_element_type=jnp.float32
    )
    return (
        grad_once.astype(jnp.bfloat16).reshape(row_count, -1),
        grad_twice.astype(jnp.bfloat16).reshape(row_count, -1),
    )


def tile_probs(rows_emb, cols_emb, row_max, row_total):
    scores = jnp.einsum("ei,ej->ij", rows_emb, cols_emb, precision=highest)
    shares = jnp.exp(jnp.maximum(scores, 0.0) - row_max[:, None]) / row_total[:, None]
    return (scores, shares)


def pair_dot(left, right):
    return lax.dot_general(
        left, right, (((1,), (1,)), ((), ())), preferred_element_type=jnp.float32
    )


def in_blocks(step_fn, status, members, axis_dim):
    amount = members[0].shape[axis_dim]
    span_size = math.gcd(amount, 512)

    def advance(position, current):
        opening = position * span_size
        sliced = tuple(
            (lax.dynamic_slice_in_dim(member, opening, span_size, axis_dim) for member in members)
        )
        return step_fn(current, sliced, opening)

    return lax.fori_loop(0, amount // span_size, advance, status)


def score_grads(status, emb_src, cols_dst, offset, scores, shares, dweights):
    grad_rows, grad_cols = status
    dscore = jnp.where(scores > 0.0, shares * dweights, 0.0)
    grad_rows = grad_rows + jnp.einsum("ej,ij->ei", cols_dst, dscore, precision=highest)
    span_size = dscore.shape[1]
    current = lax.dynamic_slice_in_dim(grad_cols, offset, span_size, 1)
    added = current + jnp.einsum("ei,ij->ej", emb_src, dscore, precision=highest)
    return (grad_rows, lax.dynamic_update_slice_in_dim(grad_cols, added, offset, 1))


def per_device(
    series, starts, sensor_order, emb_src, emb_dst, start_proj, conv_weight, mix_weight, out_grad
):
    local_rows = sensor_order.shape[0]
    embed_dim = emb_src.shape[0]
    channels = start_proj.shape[1]
    all_rows = local_rows * lax.axis_size("sensor")
    windows = jax.vmap(lambda first_step: lax.dynamic_slice_in_dim(series, first_step, STEPS, 0))(
        starts
    )
    flat_windows = windows.reshape(-1, local_rows)
    window_rows = flat_windows.shape[0]

    def pick_step(status, members, offset):
        readings_sum, dst_all = status
        block_windows, block_dst = members
        span_size = block_windows.shape[1]
        onehot = (sensor_order[:, None] == offset + lax.iota(jnp.int32, span_size)[None, :]).astype(
            jnp.float32
        )
        readings_sum = readings_sum + jnp.einsum(
            "wj,pj->wp", block_windows, onehot, precision=highest
        )
        return (readings_sum, lax.dynamic_update_slice_in_dim(dst_all, block_dst, offset, 1))

    readings_sum, dst_all = in_blocks(
        pick_step,
        (
            jnp.zeros((window_rows, local_rows), jnp.float32),
            jnp.zeros((embed_dim, all_rows), jnp.float32),
        ),
        (
            lax.all_gather(flat_windows, "sensor", axis=1, tiled=True),
            lax.all_gather(emb_dst, "sensor", axis=1, tiled=True),
        ),
        1,
    )
    readings = readings_sum.T.reshape(local_rows, -1, STEPS)
    hidden, residual = front(readings, start_proj, conv_weight)
    feat_cols = hidden.shape[1]
    span_all = math.gcd(all_rows, 512)

    def stat_step(position, current):
        best_score, summed = current
        cols_dst = lax.dynamic_slice_in_dim(dst_all, position * span_all, span_all, 1)
        scores = jnp.maximum(jnp.einsum("ei,ej->ij", emb_src, cols_dst, precision=highest), 0.0)
        new_best = jnp.maximum(best_score, jnp.max(scores, axis=1))
        summed = summed * jnp.exp(best_score - new_best) + jnp.sum(
            jnp.exp(scores - new_best[:, None]), axis=1
        )
        return (new_best, summed)

    row_max, row_total = lax.fori_loop(
        0,
        all_rows // span_all,
        stat_step,
        (jnp.zeros((local_rows,), jnp.float32), jnp.zeros((local_rows,), jnp.float32)),
    )
    grad_once, grad_twice = channel_grads(out_grad, mix_weight)

    def spread_step(status, members, offset):
        block_feat = members[0]
        cols_dst = lax.dynamic_slice_in_dim(dst_all, offset, block_feat.shape[0], 1)
        scores, shares = tile_probs(emb_src, cols_dst, row_max, row_total)
        return status + jnp.dot(
            shares.astype(jnp.bfloat16), block_feat, preferred_element_type=jnp.float32
        )

    first_init = jnp.zeros((local_rows, feat_cols), jnp.float32)
    first_result = in_blocks(
        spread_step, first_init, (lax.all_gather(hidden, "sensor", axis=0, tiled=True),), 0
    )
    diffused = first_result.astype(jnp.bfloat16)

    def plain_step(status, members, offset):
        accumulated, grad_rows, grad_cols = status
        return (spread_step(accumulated, members, offset), grad_rows, grad_cols)

    second_init = (
        jnp.zeros((local_rows, feat_cols), jnp.float32),
        jnp.zeros((embed_dim, local_rows), jnp.float32),
        jnp.zeros((embed_dim, all_rows), jnp.float32),
    )
    second_result = in_blocks(
        plain_step, second_init, (lax.all_gather(diffused, "sensor", axis=0, tiled=True),), 0
    )
    second_full, grad_rows, grad_cols = second_result
    second = second_full.astype(jnp.bfloat16)
    layer_out, stacked = mixing(residual, hidden, diffused, second, mix_weight)
    mix_part = lax.dot_general(
        stacked,
        out_grad.reshape(-1, channels),
        (((0,), (0,)), ((), ())),
        preferred_element_type=jnp.float32,
    )
    span_size = math.gcd(lax.axis_size("sensor") * local_rows, 512)

    def piece_term(position):
        cols_dst = lax.dynamic_slice_in_dim(dst_all, position * span_size, span_size, 1)
        scores, shares = tile_probs(emb_src, cols_dst, row_max, row_total)
        return lax.dot_general(
            shares.astype(jnp.bfloat16),
            grad_twice,
            (((0,), (0,)), ((), ())),
            preferred_element_type=jnp.float32,
        )

    adjoint_sum = lax.psum_scatter(
        lax.map(
            piece_term,
            jnp.arange(lax.axis_size("sensor") * local_rows // span_size, dtype=jnp.int32),
        ).reshape(lax.axis_size("sensor") * local_rows, -1),
        "sensor",
        scatter_dimension=0,
        tiled=True,
    )
    carried = (grad_once.astype(jnp.float32) + adjoint_sum).astype(jnp.bfloat16)
    row_delta = jnp.sum(
        grad_twice.astype(jnp.float32) * second_full + carried.astype(jnp.float32) * first_result,
        axis=1,
    )

    def pair_step(status, members, offset):
        block_hidden, block_diff = members
        cols_dst = lax.dynamic_slice_in_dim(dst_all, offset, block_hidden.shape[0], 1)
        scores, shares = tile_probs(emb_src, cols_dst, row_max, row_total)
        dweights = (
            pair_dot(grad_twice, block_diff) + pair_dot(carried, block_hidden) - row_delta[:, None]
        )
        return score_grads(status, emb_src, cols_dst, offset, scores, shares, dweights)

    grad_rows, grad_cols = in_blocks(
        pair_step,
        (grad_rows, grad_cols),
        (
            lax.all_gather(hidden, "sensor", axis=0, tiled=True),
            lax.all_gather(diffused, "sensor", axis=0, tiled=True),
        ),
        0,
    )
    grad_dst = lax.psum_scatter(grad_cols, "sensor", scatter_dimension=1, tiled=True)
    grad_mix = lax.psum(mix_part, "sensor")
    return (layer_out, grad_rows, grad_dst, grad_mix)


def solution(mesh):
    placed = (
        P(None, ("groups", "sensor")),
        P("groups"),
        P(("groups", "sensor")),
        P(None, ("groups", "sensor")),
        P(None, ("groups", "sensor")),
        P(),
        P(),
        P(),
        P(("groups", "sensor"), None),
    )
    return jax.shard_map(
        per_device,
        mesh=mesh,
        in_specs=placed,
        out_specs=(
            P(("groups", "sensor"), None),
            P(None, ("groups", "sensor")),
            P(None, ("groups", "sensor")),
            P("groups", None),
        ),
        check_vma=False,
    )
```

profile of v0, /device:TPU:0, one launch (start us, length us, event | category | flops | bytes accessed | tf_op | source)
XLA Modules:
  0.0 194.4 jit_solution(2964574075094498716)
XLA Ops:
  8.2 23.4 %all-gather = f32[16,48,12]{1,2,0:T(8,128)S(1)} all-gather(f32[1,48,12]{1,2,0:T(8,128)S(1)} %bitcast.98), channel_id=1, replica_groups=mesh['groups'=2,'sensor'=16] {'sensor'}, dimensions={0}, use_global_device_ids=true | all-gather | bytes 39168 | tf_op jit(solution)/shard_map/all_gather | solution.py:127
  31.8 18.0 %all-gather.1 = f32[16,48,10]{1,2,0:T(8,128)S(1)} all-gather(f32[1,48,10]{1,2,0:T(8,128)} %bitcast.100), channel_id=1, replica_groups=mesh['groups'=2,'sensor'=16] {'sensor'}, dimensions={0}, use_global_device_ids=true | all-gather | bytes 32640 | tf_op jit(solution)/shard_map/all_gather | solution.py:128
  50.0 2.7 %while.88 = (s32[]{:T(128)}, f32[12,48]{1,0:T(8,128)S(1)}, f32[10,768]{1,0:T(8,128)S(1)}, f32[12,768]{1,0:T(8,128)S(1)}, s32[48]{0:T(128)}, /*index=5*/f32[10,76...) while((s32[]{:T(128)}, f32[12,48]{1,0:T(8,128)S(1)}, f32[10,768]{1,0:T(8,128)S(1)}, ...), condition=%wide.region_1.0_spmd.clone, body=%wide.region_0.0_spmd.clone.sunk | while | flops 1783175 | bytes 62065 | solution.py:82
  50.0 0.8 convolution_add_fusion.10
  50.9 0.8 convolution_add_fusion.10
  51.9 0.8 convolution_add_fusion.10
  52.7 1.8 while.89
  55.3 7.5 %while.87 = (s32[]{:T(128)}, f32[3,256,384]{2,1,0:T(8,128)}, s32[3]{0:T(128)S(1)}, f32[10,768]{1,0:T(8,128)S(1)}, f32[10,48]{1,0:T(8,128)S(1)}, /*index=5*/f32[4...) while((s32[]{:T(128)}, f32[3,256,384]{2,1,0:T(8,128)}, ...), condition=%wide.region_11.12_spmd, body=%wide.region_10.11_spmd.sunk | while | flops 10960902 | bytes 505023 | solution.py:203
  55.3 0.6 dynamic_slice.136
  56.8 1.0 fusion.124
  57.8 0.6 dynamic_slice.136
  59.3 1.0 fusion.124
  61.8 1.0 fusion.124
  65.1 20.4 %all_gather.16 = bf16[768,384]{1,0:T(8,128)(2,1)S(1)} all-gather(bf16[48,384]{1,0:T(8,128)(2,1)S(1)} %reshape.86), channel_id=1, replica_groups=mesh['groups'=2,'sensor'=16] {'sensor'}, dimensions={0}, use_global_device_ids=true | all-gather | bytes 626688 | tf_op jit(solution)/shard_map/all_gather | solution.py:165
  85.5 1.4 while.90
  87.7 20.1 %all_gather.17 = bf16[768,384]{1,0:T(8,128)(2,1)S(1)} all-gather(bf16[48,384]{1,0:T(8,128)(2,1)S(1)} %convert_element_type.68), channel_id=1, replica_groups=mesh['groups'=2,'sensor'=16] {'sensor'}, dimensions={0}, use_global_device_ids=true | all-gather | bytes 626688 | tf_op jit(solution)/shard_map/all_gather | solution.py:179
  107.9 1.4 while.91
  109.2 12.6 %reduce-scatter.5.cloned.1.call-done = f32[48,384]{1,0:T(8,128)} async-done(((f32[768,384]{1,0:T(8,128)}), f32[48,384]{1,0:T(8,128)}) %reduce-scatter.5.cloned.1.call-update) | async-done | bytes 73744 | tf_op jit(solution)/shard_map/reduce_scatter | solution.py:202
  121.9 1.0 add_reduce_fusion
  123.2 3.0 %while.92 = (s32[]{:T(128)}, f32[10,48]{1,0:T(8,128)S(1)}, f32[10,768]{1,0:T(8,128)S(1)}, f32[10,768]{1,0:T(8,128)S(1)}, f32[10,48]{1,0:T(8,128)S(1)}, /*index=5...) while((s32[]{:T(128)}, f32[10,48]{1,0:T(8,128)S(1)}, ...), condition=%wide.region_15.16_spmd.clone, body=%wide.region_14.15_spmd.clone.sunk | while | flops 23399876 | bytes 904809 | solution.py:82
  126.2 0.9 copy.46
  127.7 0.8 reshape.89
  128.5 57.7 %psum.7 = f32[96,32]{0,1:T(8,128)} all-reduce(f32[96,32]{0,1:T(8,128)S(1)} %fusion.55), channel_id=1, replica_groups=mesh['groups'=2,'sensor'=16] {'sensor'}, use_global_device_ids=true, to_apply=%region_17.18 | all-reduce | flops 3072 | bytes 24576 | tf_op jit(solution)/shard_map/psum | solution.py:236
  186.1 1.4 copy.47
  (115 shorter events, 13.7 us)
Async XLA Ops:
  7.2 0.9 copy-start
  7.2 45.6 %copy-start.1 = (f32[10,48]{1,0:T(8,128)S(1)}, f32[10,48]{1,0:T(8,128)}, u32[]{:S(2)}) copy-start(f32[10,48]{1,0:T(8,128)} %param.24) | copy-start | bytes 5764
  7.2 114.7 %reduce-scatter.5.cloned.1.call-start = ((), (), s32[]{:S(2)}) async-start(), calls=%async_computation.2 | async-start | bytes 1253376 | tf_op jit(solution)/shard_map/reduce_scatter | solution.py:202
  31.7 22.8 %copy-start.3 = (bf16[48,384]{1,0:T(8,128)(2,1)S(1)}, bf16[48,384]{1,0:T(8,128)(2,1)}, u32[]{:S(2)}) copy-start(bf16[48,384]{1,0:T(8,128)(2,1)} %param.29) | copy-start | bytes 110596
  31.8 22.9 %copy-start.4 = (bf16[96,32]{0,1:T(8,128)(2,1)S(1)}, bf16[96,32]{0,1:T(8,128)(2,1)}, u32[]{:S(2)}) copy-start(bf16[96,32]{0,1:T(8,128)(2,1)} %param.28) | copy-start | bytes 18436
  62.8 0.7 copy-start.6
  62.8 123.3 %reduce-scatter.7.cloned.1.call-start = ((), (), s32[]{:S(2)}) async-start(), calls=%async_computation.3 | async-start | bytes 417792
  63.8 0.7 copy-start.5
  126.2 61.3 %copy-start.2 = (f32[10,48]{1,0:T(8,128)}, f32[10,48]{1,0:T(8,128)S(1)}, u32[]{:S(2)}) copy-start(f32[10,48]{1,0:T(8,128)S(1)} %get-tuple-element.696) | copy-start | bytes 5764
Sparse Core Ops, SparseCore 0:
  62.9 58.8 reduce-scatter.4
  127.3 54.7 reduce-scatter.6
where the time goes:
time: 195 us; the launch traced here: 194 us
  blocking collectives  140 us (72%)
  between operations  15 us (8%)
  matrix products  13.9 us (7%)
  waiting for transfers between devices  12.7 us (7%)
  local copies, waits for them, and re-layouts  8.47 us (4%)
  loops' own time  2.58 us (1%)
  other arithmetic  2.1 us (1%)
    psum x1, blocking collectives, per_device(): grad_mix = lax.psum(mix_part, 'sensor')  57.7 us
    all_gather x1, blocking collectives, per_device(): lax.all_gather(flat_windows, 'sensor', axis=1, tiled=True)  23.4 us
    all_gather x1, blocking collectives, per_device(): lax.all_gather(hidden, 'sensor', axis=0, tiled=True)  20.4 us
    all_gather x1, blocking collectives, per_device(): lax.all_gather(diffused, 'sensor', axis=0, tiled=True)  20.1 us
    all_gather x1, blocking collectives, per_device(): lax.all_gather(emb_dst, 'sensor', axis=1, tiled=True)  18 us
    reduce_scatter x1, waiting for transfers between devices, per_device(): lax.psum_scatter(lax.map(piece_term, jnp.arange(lax.axis_size('sensor') *...  12.6 us
  transfers between devices with their start and end apart: 2, of which 1 were waited for; matrix products, arithmetic and copies ran while one was open for 3% of the time, Pallas kernels for 0%

commit v1 on v0

--- a/solution.py
+++ b/solution.py
@@ -3,6 +3,8 @@
 import jax
 import jax.numpy as jnp
 from jax import lax
+from jax.experimental import pallas as pl
+from jax.experimental.pallas import tpu as pltpu
 from jax.sharding import PartitionSpec as P
 
 STEPS = 12
@@ -237,6 +239,352 @@
     return (layer_out, grad_rows, grad_dst, grad_mix)
 
 
+PIECE = 16
+QUARTERS = 3
+NT = (((1,), (1,)), ((), ()))
+TN = (((0,), (0,)), ((), ()))
+f32 = jnp.float32
+bf16 = jnp.bfloat16
+
+
+def iota(shape, dim):
+    return lax.broadcasted_iota(jnp.int32, shape, dim)
+
+
+def ones_where(mask):
+    return jnp.where(mask, 1.0, 0.0).astype(bf16)
+
+
+def nn(left, right):
+    return jnp.dot(left, right, preferred_element_type=f32)
+
+
+def nt(left, right):
+    return lax.dot_general(left, right, NT, preferred_element_type=f32)
+
+
+def tn(left, right):
+    return lax.dot_general(left, right, TN, preferred_element_type=f32)
+
+
+def halves(value):
+    high = value.astype(bf16)
+    return high, (value - high.astype(f32)).astype(bf16)
+
+
+def thirds(value):
+    high, middle = halves(value)
+    return high, middle, (value - high.astype(f32) - middle.astype(f32)).astype(bf16)
+
+
+def selection(q):
+    col = iota((1, 384), 1)
+    tile, lane = col >> 7, col & 127
+    u, e = lane >> 4, lane & 15
+    left = jnp.where((u == 2) | (u == 5), 1, jnp.where(u == 4, 2, 0)) * 128 + e
+    right = jnp.where((u == 1) | (u == 5), 1, jnp.where(u == 3, 2, 0)) * 128 + e + 10
+    window = u * 128 + e + 20
+    wanted = jnp.where(tile == 0, left, jnp.where(tile == 1, right, window))
+    blocks, width = jnp.where(tile == 2, 3, 6), jnp.where(tile == 2, 12, 10)
+    wanted = jnp.where((u < blocks) & (e < width), wanted + 40 * q, -1)
+    number = jnp.where(col == 320, 32 + 40 * q, -1)
+    row = iota((384, 384), 0)
+    return ones_where((row == wanted) | ((row & 127) == number))
+
+
+def layer_kernel(
+    n, starts, series, order, src, dst, start_proj, conv, mix, out_grad,
+    layer_out, grad_src, grad_dst, grad_mix,
+    packed, small, grads, left_emb, right_emb, window_f, window_b, hidden, residual,
+    adj, diff_full, diffused, second_full, second, once, twice, carried, stats,
+    small_send, small_recv, big_send, big_recv, pass_send, pass_recv,
+):
+    me = lax.axis_index("sensor")
+    rows_q = PIECE * n
+    total = QUARTERS * rows_q
+    barrier = pltpu.get_barrier_semaphore()
+    for k in range(1, n):
+        pl.semaphore_signal(
+            barrier, inc=1, device_id={"sensor": lax.rem(me + k, n)},
+            device_id_type=pl.DeviceIdType.MESH,
+        )
+    mine = pl.multiple_of(me * PIECE, PIECE)
+
+    window = series[pl.ds(starts[0], STEPS), :]
+    block = jnp.concatenate(
+        [src[...], dst[...], window, order[...].astype(f32), jnp.zeros((7, 48), f32)], axis=0
+    )
+    packed[...] = jnp.zeros_like(packed)
+    for q in range(QUARTERS):
+        packed[40 * q : 40 * q + 40, 0:PIECE] = block[:, PIECE * q : PIECE * (q + 1)]
+    small[pl.ds(mine, PIECE), :] = packed[...].T[0:PIECE, :]
+    for q in range(QUARTERS):
+        grads[q, pl.ds(mine, PIECE), :] = out_grad[PIECE * q : PIECE * (q + 1), :]
+
+    pl.semaphore_wait(barrier, n - 1)
+
+    def remote(where, send, recv, peer):
+        return pltpu.make_async_remote_copy(
+            src_ref=where, dst_ref=where, send_sem=send, recv_sem=recv,
+            device_id={"sensor": peer}, device_id_type=pl.DeviceIdType.MESH,
+        )
+
+    small_copies = []
+    for k in range(1, n):
+        copy = remote(
+            small.at[pl.ds(mine, PIECE), :], small_send.at[k], small_recv.at[k],
+            lax.rem(me + k, n),
+        )
+        copy.start()
+        small_copies.append(copy)
+    sibling = me + 1 - 2 * lax.rem(me, 2)
+    big_copies = []
+    for k in range(n // 2):
+        copy = remote(
+            grads.at[:, pl.ds(mine, PIECE), :], big_send.at[k], big_recv.at[k],
+            sibling if k == 0 else lax.rem(me + 2 * k, n),
+        )
+        copy.start()
+        big_copies.append(copy)
+
+    spread = ones_where(iota((256, 64), 1) == (iota((256, 64), 0) >> 7) * 32 + (iota((256, 64), 0) & 31))
+    gather = ones_where(iota((64, 256), 0) == (iota((64, 256), 1) >> 7) * 32 + (iota((64, 256), 1) & 31))
+    conv_big = nn(nn(spread, conv[...]).astype(bf16), gather)
+    conv_big = jnp.where(
+        ((iota((256, 256), 0) & 127) >> 5) == ((iota((256, 256), 1) & 127) >> 5), conv_big, 0.0
+    ).astype(bf16)
+    spread = ones_where(iota((384, 96), 1) == (iota((384, 96), 0) >> 7) * 32 + (iota((384, 96), 0) & 31))
+    gather = ones_where(iota((32, 128), 0) == (iota((32, 128), 1) & 31))
+    mix_big = nn(nn(spread, mix[...]).astype(bf16), gather)
+    mix_big = jnp.where(
+        ((iota((384, 128), 0) & 127) >> 5) == (iota((384, 128), 1) >> 5), mix_big, 0.0
+    ).astype(bf16)
+    proj = jnp.concatenate([start_proj[...]] * 4, axis=1)
+    weight, bias = proj[0:1, :], proj[1:2, :]
+    at = iota((128, 768), 0)
+    col = iota((128, 768), 1)
+    step = jnp.where(col < 384, (col >> 5) - 1, (col - 384) >> 5)
+    expand = ones_where(((at & 15) == step) & (at < 48))
+    numbers = jnp.concatenate(
+        [
+            48 * (iota((1, rows_q), 1) >> 4) + PIECE * q + (iota((1, rows_q), 1) & 15)
+            for q in range(QUARTERS)
+        ],
+        axis=1,
+    ).astype(f32)
+
+    for copy in small_copies:
+        copy.wait_recv()
+
+    parts = jnp.concatenate(thirds(small[...]), axis=1)
+    for q in range(QUARTERS):
+        taken = nn(parts, selection(q))
+        rows = slice(q * rows_q, (q + 1) * rows_q)
+        left_emb[rows, :] = taken[:, 0:128].astype(bf16)
+        right_emb[rows, :] = taken[:, 128:256].astype(bf16)
+        window_f[rows, :] = taken[:, 256:384]
+        window_b[rows, :] = taken[:, 256:384].astype(bf16)
+
+    def chunk(q):
+        return pl.ds(pl.multiple_of(q * rows_q, rows_q), rows_q)
+
+    def front_step(q, carry):
+        rows = chunk(q)
+        onehot = ones_where(window_f[rows, 64:65] == numbers)
+        picked = nn(onehot, window_b[...]).astype(bf16)
+        wide = nn(picked, expand)
+        for b in range(3):
+            lanes = slice(128 * b, 128 * (b + 1))
+            before = (wide[:, 128 * b : 128 * (b + 1)] * weight + bias).astype(bf16)
+            after = (wide[:, 384 + 128 * b : 512 + 128 * b] * weight + bias).astype(bf16)
+            residual[rows, lanes] = after
+            terms = nn(jnp.concatenate([before, after], axis=1), conv_big)
+            gated = jnp.tanh(terms[:, :128]) * (0.5 * jnp.tanh(0.5 * terms[:, 128:]) + 0.5)
+            hidden[rows, lanes] = gated.astype(bf16)
+        return carry
+
+    lax.fori_loop(0, QUARTERS, front_step, 0)
+
+    def first_step(q, carry):
+        rows = chunk(q)
+        positive = jnp.maximum(nt(left_emb[rows, :], right_emb[...]), 0.0)
+        top = jnp.max(positive, axis=1, keepdims=True)
+        terms = jnp.exp(positive - top)
+        inverse = 1.0 / jnp.sum(terms, axis=1, keepdims=True)
+        weights = (terms * inverse).astype(bf16)
+        adj[rows, :] = weights
+        stats[rows, 0:1] = top
+        stats[rows, 1:2] = inverse
+        result = nn(weights, hidden[...])
+        diff_full[rows, :] = result
+        diffused[rows, :] = result.astype(bf16)
+        return carry
+
+    lax.fori_loop(0, QUARTERS, first_step, 0)
+
+    pass_copies = []
+    for k in range(1, n // 2):
+        big_copies[k].wait_recv()
+        origin = pl.multiple_of(lax.rem(me + n - 2 * k, n) * PIECE, PIECE)
+        copy = remote(
+            grads.at[:, pl.ds(origin, PIECE), :], pass_send.at[k], pass_recv.at[k], sibling
+        )
+        copy.start()
+        pass_copies.append(copy)
+
+    def second_step(q, carry):
+        rows = chunk(q)
+        result = nn(adj[rows, :], diffused[...])
+        second_full[rows, :] = result
+        second[rows, :] = result.astype(bf16)
+        return carry
+
+    lax.fori_loop(0, QUARTERS, second_step, 0)
+
+    big_copies[0].wait_recv()
+    for copy in pass_copies:
+        copy.wait_recv()
+
+    def channel_step(q, carry):
+        rows = chunk(q)
+        given = grads[q]
+        for b in range(3):
+            lanes = slice(128 * b, 128 * (b + 1))
+            both = nt(given[:, lanes], mix_big[128:384, :]).astype(bf16)
+            once[rows, lanes] = both[:, :128]
+            twice[rows, lanes] = both[:, 128:]
+        return carry
+
+    lax.fori_loop(0, QUARTERS, channel_step, 0)
+
+    def adjoint_step(q, carry):
+        rows = chunk(q)
+        back = tn(adj[:, rows], twice[...])
+        total_grad = (once[rows, :].astype(f32) + back).astype(bf16)
+        carried[rows, :] = total_grad
+        delta = twice[rows, :].astype(f32) * second_full[rows, :] + total_grad.astype(
+            f32
+        ) * diff_full[rows, :]
+        stats[rows, 2:3] = jnp.sum(delta, axis=1, keepdims=True)
+        return carry
+
+    lax.fori_loop(0, QUARTERS, adjoint_step, 0)
+
+    def own(ref):
+        return jnp.concatenate(
+            [
+                ref[pl.ds(pl.multiple_of(q * rows_q + me * PIECE, PIECE), PIECE), :]
+                for q in range(QUARTERS)
+            ],
+            axis=0,
+        )
+
+    own_hidden, own_diff, own_second = own(hidden), own(diffused), own(second)
+    own_left, own_right, own_stats = own(left_emb), own(right_emb), own(stats)
+    own_residual = own(residual)
+    for b in range(3):
+        lanes = slice(128 * b, 128 * (b + 1))
+        features = jnp.concatenate(
+            [own_hidden[:, lanes], own_diff[:, lanes], own_second[:, lanes]], axis=1
+        )
+        layer_out[:, lanes] = (own_residual[:, lanes].astype(f32) + nn(features, mix_big)).astype(
+            bf16
+        )
+
+    def score_grad(scores, stat, products):
+        shares = jnp.exp(jnp.maximum(scores, 0.0) - stat[:, 0:1]) * stat[:, 1:2]
+        return halves(jnp.where(scores > 0.0, shares * (products - stat[:, 2:3]), 0.0))
+
+    high, low = score_grad(
+        nt(own_left, right_emb[...]),
+        own_stats,
+        nt(own(twice), diffused[...]) + nt(own(carried), hidden[...]),
+    )
+    summed = (nn(high, right_emb[...]) + nn(low, right_emb[...])).T
+    grad_src[...] = summed[0:10, :] + summed[16:26, :] + summed[48:58, :]
+
+    high, low = score_grad(
+        nt(left_emb[...], own_right),
+        stats[...],
+        nt(twice[...], own_diff) + nt(carried[...], own_hidden),
+    )
+    summed = tn(left_emb[...], high) + tn(left_emb[...], low)
+    grad_dst[...] = summed[0:10, :] + summed[32:42, :] + summed[64:74, :]
+
+    mixed = jnp.zeros((128, 384), f32)
+    for b in range(3):
+        lanes = slice(128 * b, 128 * (b + 1))
+        features = jnp.concatenate([hidden[:, lanes], diffused[:, lanes], second[:, lanes]], axis=1)
+        mixed = mixed + tn(grads[:, :, lanes].reshape(total, 128), features)
+    mixed = mixed.T
+    for k in range(3):
+        grad_mix[32 * k : 32 * (k + 1), :] = sum(
+            mixed[128 * k + 32 * t : 128 * k + 32 * (t + 1), 32 * t : 32 * (t + 1)]
+            for t in range(4)
+        )
+
+    for copy in small_copies + big_copies + pass_copies:
+        copy.wait_send()
+
+
+def whole_in_kernel(
+    series, starts, sensor_order, emb_src, emb_dst, start_proj, conv_weight, mix_weight, out_grad
+):
+    n = lax.axis_size("sensor")
+    total = 48 * n
+    vmem = pl.BlockSpec(memory_space=pltpu.VMEM)
+    dma = pltpu.SemaphoreType.DMA
+    return pl.pallas_call(
+        lambda *refs: layer_kernel(n, *refs),
+        out_shape=(
+            jax.ShapeDtypeStruct((48, 384), bf16),
+            jax.ShapeDtypeStruct((10, 48), f32),
+            jax.ShapeDtypeStruct((10, 48), f32),
+            jax.ShapeDtypeStruct((96, 32), f32),
+        ),
+        in_specs=[pl.BlockSpec(memory_space=pltpu.SMEM)] + [vmem] * 8,
+        out_specs=(vmem,) * 4,
+        scratch_shapes=[
+            pltpu.VMEM((128, 128), f32),
+            pltpu.VMEM((PIECE * n, 128), f32),
+            pltpu.VMEM((QUARTERS, PIECE * n, 384), bf16),
+            pltpu.VMEM((total, 128), bf16),
+            pltpu.VMEM((total, 128), bf16),
+            pltpu.VMEM((total, 128), f32),
+            pltpu.VMEM((total, 128), bf16),
+            pltpu.VMEM((total, 384), bf16),
+            pltpu.VMEM((total, 384), bf16),
+            pltpu.VMEM((total, total), bf16),
+            pltpu.VMEM((total, 384), f32),
+            pltpu.VMEM((total, 384), bf16),
+            pltpu.VMEM((total, 384), f32),
+            pltpu.VMEM((total, 384), bf16),
+            pltpu.VMEM((total, 384), bf16),
+            pltpu.VMEM((total, 384), bf16),
+            pltpu.VMEM((total, 384), bf16),
+            pltpu.VMEM((total, 128), f32),
+            dma((n,)),
+            dma((n,)),
+            dma((n // 2,)),
+            dma((n // 2,)),
+            dma((n // 2,)),
+            dma((n // 2,)),
+        ],
+        compiler_params=pltpu.CompilerParams(
+            collective_id=0, has_side_effects=True, vmem_limit_bytes=48 * 2**20
+        ),
+    )(
+        starts, series, sensor_order.reshape(1, -1), emb_src, emb_dst, start_proj, conv_weight,
+        mix_weight, out_grad,
+    )
+
+
+def layer_on_device(*operands):
+    if lax.axis_size("sensor") == 16 and operands[2].shape[0] == 48:
+        return whole_in_kernel(*operands)
+    return per_device(*operands)
+
+
 def solution(mesh):
     placed = (
         P(None, ("groups", "sensor")),
@@ -250,7 +598,7 @@
         P(("groups", "sensor"), None),
     )
     return jax.shard_map(
-        per_device,
+        layer_on_device,
         mesh=mesh,
         in_specs=placed,
         out_specs=(

time: 195 us -> 28.7 us (0.15)
  the two profiles are of different devices: /device:TPU:0 before, /device:TPU:13 now
where the time goes in v1:
time: 28.7 us; the launch traced here: 28.4 us
  Pallas kernels  22.7 us (79%)
  local copies, waits for them, and re-layouts  4.34 us (15%)
  between operations  1.39 us (5%)
    pallas_call x1, Pallas kernels, whole_in_kernel(): pl.pallas_call(lambda *refs: layer_kernel(n, *refs), out_shape=(jax.Shape...  22.7 us
    unnamed x17, local copies, waits for them, and re-layouts  3.66 us
    pallas_call x1, local copies, waits for them, and re-layouts, whole_in_kernel(): pl.pallas_call(lambda *refs: layer_kernel(n, *refs), out_shape=(jax.Shape...  0.68 us

profile of v1, /device:TPU:13, one launch (start us, length us, event | category | flops | bytes accessed | tf_op | source)
XLA Modules:
  0.0 28.4 jit_solution(12572412415219496364)
XLA Ops:
  1.3 0.8 %copy.14.refs_7_ = bf16[96,32]{1,0:T(8,128)(2,1)S(1)} copy(bf16[96,32]{0,1:T(8,128)(2,1)} %param.16) | data formatting | bytes 12288 | tf_op args[7]
  2.1 0.0 copy-start
  2.1 0.0 copy-start.1
  2.1 0.0 copy-start.2
  2.1 0.0 copy-start.3
  2.1 0.0 copy-start.4
  2.1 0.0 copy-start.5
  2.1 1.0 %copy.13.refs_1_ = f32[288,48]{1,0:T(8,128)S(1)} copy(f32[288,48]{0,1:T(8,128)} %param.9) | data formatting | bytes 110592 | tf_op args[0]
  3.2 0.0 copy-done
  3.2 0.0 copy-done.1
  3.2 0.0 copy-done.2
  3.2 0.0 copy-done.3
  3.2 0.0 copy-done.4
  3.2 0.0 copy-done.5
  3.2 22.7 %shard_map.120 = (bf16[48,384]{1,0:T(8,128)(2,1)S(1)}, f32[10,48]{1,0:T(8,128)S(1)}, f32[10,48]{1,0:T(8,128)S(1)}, f32[96,32]{1,0:T(8,128)S(1)}) custom-call(s32[1]{0:T(128)S(6)} %copy.19.refs_0_, f32[288,48]{1,0:T(8,128)S(1)} %copy.13.refs_1_, s32[1,48]{1,0:T(1,128)S(1)} %bitcast.1, f32[10,48]{1,0:T(8,128)S(1)} %copy-done.2, f32[10,48]{1,0:T(8,128)S(1)} %copy-done.3, ...), custom_call_target="tpu_custom_call" | custom-call | tf_op jit(solution)/shard_map/pallas_call | solution.py:537
  25.9 0.7 %copy.15 = f32[96,32]{0,1:T(8,128)} copy(f32[96,32]{1,0:T(8,128)S(1)} %get-tuple-element.7) | data formatting | bytes 24576 | tf_op jit(solution)/shard_map/pallas_call | solution.py:537
  26.6 0.6 %copy.20 = bf16[48,384]{1,0:T(8,128)(2,1)} copy(bf16[48,384]{1,0:T(8,128)(2,1)S(1)} %get-tuple-element.12) | data formatting | bytes 73728
  27.2 0.6 %copy.21 = f32[10,48]{1,0:T(8,128)} copy(f32[10,48]{1,0:T(8,128)S(1)} %get-tuple-element.13) | data formatting | bytes 3840
  27.8 0.6 %copy.22 = f32[10,48]{1,0:T(8,128)} copy(f32[10,48]{1,0:T(8,128)S(1)} %get-tuple-element.14) | data formatting | bytes 3840
Async XLA Ops:
  2.1 1.1 %copy-start = (bf16[48,384]{1,0:T(8,128)(2,1)S(1)}, bf16[48,384]{1,0:T(8,128)(2,1)}, u32[]{:S(2)}) copy-start(bf16[48,384]{1,0:T(8,128)(2,1)} %refs_8_.1) | copy-start | bytes 110596
  2.1 1.1 %copy-start.1 = (bf16[64,64]{1,0:T(8,128)(2,1)S(1)}, bf16[64,64]{1,0:T(8,128)(2,1)}, u32[]{:S(2)}) copy-start(bf16[64,64]{1,0:T(8,128)(2,1)} %refs_6_.1) | copy-start | bytes 24580
  2.1 1.1 %copy-start.2 = (f32[10,48]{1,0:T(8,128)S(1)}, f32[10,48]{1,0:T(8,128)}, u32[]{:S(2)}) copy-start(f32[10,48]{1,0:T(8,128)} %refs_3_.1) | copy-start | bytes 5764
  2.1 1.1 %copy-start.3 = (f32[10,48]{1,0:T(8,128)S(1)}, f32[10,48]{1,0:T(8,128)}, u32[]{:S(2)}) copy-start(f32[10,48]{1,0:T(8,128)} %refs_4_.1) | copy-start | bytes 5764
  2.1 1.1 %copy-start.4 = (f32[2,32]{1,0:T(2,128)S(1)}, f32[2,32]{1,0:T(2,128)}, u32[]{:S(2)}) copy-start(f32[2,32]{1,0:T(2,128)} %refs_5_.1) | copy-start | bytes 772
  2.1 1.1 %copy-start.5 = (s32[48]{0:T(128)S(1)}, s32[48]{0:T(128)}, u32[]{:S(2)}) copy-start(s32[48]{0:T(128)} %param.11) | copy-start | bytes 580

commit v2 on v1

--- a/solution.py
+++ b/solution.py
@@ -292,13 +292,24 @@
     return ones_where((row == wanted) | ((row & 127) == number))
 
 
-def layer_kernel(
-    n, starts, series, order, src, dst, start_proj, conv, mix, out_grad,
-    layer_out, grad_src, grad_dst, grad_mix,
-    packed, small, grads, left_emb, right_emb, window_f, window_b, hidden, residual,
-    adj, diff_full, diffused, second_full, second, once, twice, carried, stats,
-    small_send, small_recv, big_send, big_recv, pass_send, pass_recv,
+def gather_kernel(
+    n, starts, series_in, order_in, src_in, dst_in, proj_in, conv_in, mix_in, out_grad_in,
+    grads, left_emb, right_emb, hidden, residual, diffused, second, twice, carried, stats, mix_out,
+    series, order, src, dst, start_proj, conv, mix, out_grad,
+    packed, small, window_f, window_b, adj, diff_full, second_full, once,
+    load_sem, small_send, small_recv, big_send, big_recv, pass_send, pass_recv,
 ):
+    loads = [
+        pltpu.make_async_copy(source, target, load_sem.at[at])
+        for at, (source, target) in enumerate(
+            [
+                (series_in, series), (order_in, order), (src_in, src), (dst_in, dst),
+                (out_grad_in, out_grad), (conv_in, conv), (mix_in, mix), (proj_in, start_proj),
+            ]
+        )
+    ]
+    for load in loads:
+        load.start()
     me = lax.axis_index("sensor")
     rows_q = PIECE * n
     total = QUARTERS * rows_q
@@ -310,7 +321,10 @@
         )
     mine = pl.multiple_of(me * PIECE, PIECE)
 
-    window = series[pl.ds(starts[0], STEPS), :]
+    wanted = ones_where(iota((16, series.shape[1]), 1) == iota((16, series.shape[1]), 0) + starts[0])
+    for load in loads[:4]:
+        load.wait()
+    window = sum(nt(wanted, part) for part in thirds(series[...]))[0:STEPS, :]
     block = jnp.concatenate(
         [src[...], dst[...], window, order[...].astype(f32), jnp.zeros((7, 48), f32)], axis=0
     )
@@ -318,6 +332,7 @@
     for q in range(QUARTERS):
         packed[40 * q : 40 * q + 40, 0:PIECE] = block[:, PIECE * q : PIECE * (q + 1)]
     small[pl.ds(mine, PIECE), :] = packed[...].T[0:PIECE, :]
+    loads[4].wait()
     for q in range(QUARTERS):
         grads[q, pl.ds(mine, PIECE), :] = out_grad[PIECE * q : PIECE * (q + 1), :]
 
@@ -347,6 +362,9 @@
         copy.start()
         big_copies.append(copy)
 
+    for load in loads[5:]:
+        load.wait()
+
     spread = ones_where(iota((256, 64), 1) == (iota((256, 64), 0) >> 7) * 32 + (iota((256, 64), 0) & 31))
     gather = ones_where(iota((64, 256), 0) == (iota((64, 256), 1) >> 7) * 32 + (iota((64, 256), 1) & 31))
     conv_big = nn(nn(spread, conv[...]).astype(bf16), gather)
@@ -355,10 +373,11 @@
     ).astype(bf16)
     spread = ones_where(iota((384, 96), 1) == (iota((384, 96), 0) >> 7) * 32 + (iota((384, 96), 0) & 31))
     gather = ones_where(iota((32, 128), 0) == (iota((32, 128), 1) & 31))
-    mix_big = nn(nn(spread, mix[...]).astype(bf16), gather)
+    mix_big = nn(nt(spread, mix[...]).astype(bf16), gather)
     mix_big = jnp.where(
         ((iota((384, 128), 0) & 127) >> 5) == (iota((384, 128), 1) >> 5), mix_big, 0.0
     ).astype(bf16)
+    mix_out[...] = mix_big
     proj = jnp.concatenate([start_proj[...]] * 4, axis=1)
     weight, bias = proj[0:1, :], proj[1:2, :]
     at = iota((128, 768), 0)
@@ -470,6 +489,28 @@
 
     lax.fori_loop(0, QUARTERS, adjoint_step, 0)
 
+    for copy in small_copies + big_copies + pass_copies:
+        copy.wait_send()
+
+
+def finish_kernel(
+    n, grads, left_emb, right_emb, hidden, residual, diffused, second, twice, carried, stats, mix_big,
+    layer_out_to, grad_src_to, grad_dst_to, grad_mix_to,
+    layer_out, grad_src, grad_dst, grad_mix, store_sem,
+):
+    me = lax.axis_index("sensor")
+    rows_q = PIECE * n
+    total = QUARTERS * rows_q
+    stores = [
+        pltpu.make_async_copy(source, target, store_sem.at[at])
+        for at, (source, target) in enumerate(
+            [
+                (layer_out, layer_out_to), (grad_mix, grad_mix_to),
+                (grad_src, grad_src_to), (grad_dst, grad_dst_to),
+            ]
+        )
+    ]
+
     def own(ref):
         return jnp.concatenate(
             [
@@ -487,44 +528,47 @@
         features = jnp.concatenate(
             [own_hidden[:, lanes], own_diff[:, lanes], own_second[:, lanes]], axis=1
         )
-        layer_out[:, lanes] = (own_residual[:, lanes].astype(f32) + nn(features, mix_big)).astype(
+        layer_out[:, lanes] = (own_residual[:, lanes].astype(f32) + nn(features, mix_big[...])).astype(
             bf16
         )
 
-    def score_grad(scores, stat, products):
-        shares = jnp.exp(jnp.maximum(scores, 0.0) - stat[:, 0:1]) * stat[:, 1:2]
-        return halves(jnp.where(scores > 0.0, shares * (products - stat[:, 2:3]), 0.0))
-
-    high, low = score_grad(
-        nt(own_left, right_emb[...]),
-        own_stats,
-        nt(own(twice), diffused[...]) + nt(own(carried), hidden[...]),
-    )
-    summed = (nn(high, right_emb[...]) + nn(low, right_emb[...])).T
-    grad_src[...] = summed[0:10, :] + summed[16:26, :] + summed[48:58, :]
-
-    high, low = score_grad(
-        nt(left_emb[...], own_right),
-        stats[...],
-        nt(twice[...], own_diff) + nt(carried[...], own_hidden),
-    )
-    summed = tn(left_emb[...], high) + tn(left_emb[...], low)
-    grad_dst[...] = summed[0:10, :] + summed[32:42, :] + summed[64:74, :]
+    stores[0].start()
 
     mixed = jnp.zeros((128, 384), f32)
     for b in range(3):
         lanes = slice(128 * b, 128 * (b + 1))
         features = jnp.concatenate([hidden[:, lanes], diffused[:, lanes], second[:, lanes]], axis=1)
         mixed = mixed + tn(grads[:, :, lanes].reshape(total, 128), features)
-    mixed = mixed.T
     for k in range(3):
-        grad_mix[32 * k : 32 * (k + 1), :] = sum(
-            mixed[128 * k + 32 * t : 128 * k + 32 * (t + 1), 32 * t : 32 * (t + 1)]
+        grad_mix[:, 32 * k : 32 * (k + 1)] = sum(
+            mixed[32 * t : 32 * (t + 1), 128 * k + 32 * t : 128 * k + 32 * (t + 1)]
             for t in range(4)
         )
-
-    for copy in small_copies + big_copies + pass_copies:
-        copy.wait_send()
+    stores[1].start()
+
+    def score_grad(scores, stat, products):
+        shares = jnp.exp(jnp.maximum(scores, 0.0) - stat[:, 0:1]) * stat[:, 1:2]
+        return halves(jnp.where(scores > 0.0, shares * (products - stat[:, 2:3]), 0.0))
+
+    high, low = score_grad(
+        nt(own_left, right_emb[...]),
+        own_stats,
+        nt(own(twice), diffused[...]) + nt(own(carried), hidden[...]),
+    )
+    summed = (nn(high, right_emb[...]) + nn(low, right_emb[...])).T
+    grad_src[...] = summed[0:10, :] + summed[16:26, :] + summed[48:58, :]
+    stores[2].start()
+
+    high, low = score_grad(
+        nt(left_emb[...], own_right),
+        stats[...],
+        nt(twice[...], own_diff) + nt(carried[...], own_hidden),
+    )
+    summed = tn(left_emb[...], high) + tn(left_emb[...], low)
+    grad_dst[...] = summed[0:10, :] + summed[32:42, :] + summed[64:74, :]
+    stores[3].start()
+    for store in stores:
+        store.wait()
 
 
 def whole_in_kernel(
@@ -533,36 +577,36 @@
     n = lax.axis_size("sensor")
     total = 48 * n
     vmem = pl.BlockSpec(memory_space=pltpu.VMEM)
+    anywhere = pl.BlockSpec(memory_space=pltpu.HBM)
     dma = pltpu.SemaphoreType.DMA
-    return pl.pallas_call(
-        lambda *refs: layer_kernel(n, *refs),
+    wide = jax.ShapeDtypeStruct((total, 384), bf16)
+    lane = jax.ShapeDtypeStruct((total, 128), bf16)
+    operands = (
+        series.T, sensor_order.reshape(1, -1), emb_src, emb_dst, start_proj, conv_weight,
+        mix_weight.T, out_grad,
+    )
+    operands = tuple(pltpu.with_memory_space_constraint(operand, pltpu.HBM) for operand in operands)
+    held = pl.pallas_call(
+        lambda *refs: gather_kernel(n, *refs),
         out_shape=(
-            jax.ShapeDtypeStruct((48, 384), bf16),
-            jax.ShapeDtypeStruct((10, 48), f32),
-            jax.ShapeDtypeStruct((10, 48), f32),
-            jax.ShapeDtypeStruct((96, 32), f32),
+            jax.ShapeDtypeStruct((QUARTERS, PIECE * n, 384), bf16),
+            lane, lane, wide, wide, wide, wide, wide, wide,
+            jax.ShapeDtypeStruct((total, 128), f32),
+            jax.ShapeDtypeStruct((384, 128), bf16),
         ),
-        in_specs=[pl.BlockSpec(memory_space=pltpu.SMEM)] + [vmem] * 8,
-        out_specs=(vmem,) * 4,
-        scratch_shapes=[
+        in_specs=[pl.BlockSpec(memory_space=pltpu.SMEM)] + [anywhere] * 8,
+        out_specs=(vmem,) * 11,
+        scratch_shapes=[pltpu.VMEM(operand.shape, operand.dtype) for operand in operands]
+        + [
             pltpu.VMEM((128, 128), f32),
             pltpu.VMEM((PIECE * n, 128), f32),
-            pltpu.VMEM((QUARTERS, PIECE * n, 384), bf16),
-            pltpu.VMEM((total, 128), bf16),
-            pltpu.VMEM((total, 128), bf16),
             pltpu.VMEM((total, 128), f32),
             pltpu.VMEM((total, 128), bf16),
-            pltpu.VMEM((total, 384), bf16),
-            pltpu.VMEM((total, 384), bf16),
             pltpu.VMEM((total, total), bf16),
             pltpu.VMEM((total, 384), f32),
-            pltpu.VMEM((total, 384), bf16),
             pltpu.VMEM((total, 384), f32),
             pltpu.VMEM((total, 384), bf16),
-            pltpu.VMEM((total, 384), bf16),
-            pltpu.VMEM((total, 384), bf16),
-            pltpu.VMEM((total, 384), bf16),
-            pltpu.VMEM((total, 128), f32),
+            dma((8,)),
             dma((n,)),
             dma((n,)),
             dma((n // 2,)),
@@ -571,12 +615,24 @@
             dma((n // 2,)),
         ],
         compiler_params=pltpu.CompilerParams(
-            collective_id=0, has_side_effects=True, vmem_limit_bytes=48 * 2**20
+            collective_id=0, has_side_effects=True, vmem_limit_bytes=32 * 2**20
         ),
-    )(
-        starts, series, sensor_order.reshape(1, -1), emb_src, emb_dst, start_proj, conv_weight,
-        mix_weight, out_grad,
-    )
+    )(starts, *operands)
+    outs = (
+        jax.ShapeDtypeStruct((48, 384), bf16),
+        jax.ShapeDtypeStruct((10, 48), f32),
+        jax.ShapeDtypeStruct((10, 48), f32),
+        jax.ShapeDtypeStruct((32, 96), f32),
+    )
+    layer_out, grad_src, grad_dst, grad_mix = pl.pallas_call(
+        lambda *refs: finish_kernel(n, *refs),
+        out_shape=outs,
+        in_specs=[vmem] * 11,
+        out_specs=(anywhere,) * 4,
+        scratch_shapes=[pltpu.VMEM(out.shape, out.dtype) for out in outs] + [dma((4,))],
+        compiler_params=pltpu.CompilerParams(vmem_limit_bytes=32 * 2**20),
+    )(*held)
+    return layer_out, grad_src, grad_dst, grad_mix.T
 
 
 def layer_on_device(*operands):

time: 28.7 us -> 24.7 us (0.86)
  local copies, waits for them, and re-layouts: 4.34 us -> 0 us
  Pallas kernels: 22.7 us -> 23.3 us
    unnamed x17 -> x0, local copies, waits for them, and re-layouts: 3.66 us -> none
    pallas_call x1 -> x0, local copies, waits for them, and re-layouts: 0.68 us -> none  [whole_in_kernel(): pl.pallas_call(lambda *refs: layer_kernel(n, *refs), out_shape=(jax.Shape...]
    pallas_call x1 -> x2, Pallas kernels: 22.7 us -> 23.3 us  [the longest x1 20.9 us: whole_in_kernel(): pl.pallas_call(lambda *refs: gather_kernel(n, *refs), out_shape=(jax.Shap...]
where the time goes in v2:
time: 24.7 us; the launch traced here: 24.6 us
  Pallas kernels  23.3 us (94%)
  between operations  1.29 us (5%)
    pallas_call x1, Pallas kernels, whole_in_kernel(): pl.pallas_call(lambda *refs: gather_kernel(n, *refs), out_shape=(jax.Shap...  20.9 us
    pallas_call x1, Pallas kernels, whole_in_kernel(): pl.pallas_call(lambda *refs: finish_kernel(n, *refs), out_shape=outs, in_...  2.42 us

profile of v2, /device:TPU:13, one launch (start us, length us, event | category | flops | bytes accessed | tf_op | source)
XLA Modules:
  0.0 24.6 jit_solution(5192795690911625891)
XLA Ops:
  1.3 20.9 %shard_map.120 = (bf16[3,256,384]{2,1,0:T(8,128)(2,1)S(1)}, bf16[768,128]{1,0:T(8,128)(2,1)S(1)}, bf16[768,128]{1,0:T(8,128)(2,1)S(1)}, bf16[768,384]{1,0:T(8,12...) custom-call(s32[1]{0:T(128)S(6)} %copy.13.refs_0_, ...), custom_call_target="tpu_custom_call" | custom-call | tf_op jit(solution)/shard_map/pallas_call | solution.py:589
  22.1 2.4 %shard_map.121 = (bf16[48,384]{1,0:T(8,128)(2,1)}, f32[10,48]{1,0:T(8,128)}, f32[10,48]{1,0:T(8,128)}, f32[32,96]{1,0:T(8,128)}) custom-call(bf16[3,256,384]{2,1,0:T(8,128)(2,1)S(1)} %get-tuple-element.19.refs_0_, bf16[768,128]{1,0:T(8,128)(2,1)S(1)} %get-tuple-element.20.refs_1_, bf16[768,128]{1,0:T(8,128)(2,1)S(1)} %get-tuple-element.21.refs_2_, ...), custom_call_target="tpu_custom_call" | custom-call | tf_op jit(solution)/shard_map/pallas_call | solution.py:627

commit v3 on v2

--- a/solution.py
+++ b/solution.py
@@ -345,14 +345,14 @@
         )
 
     small_copies = []
-    for k in range(1, n):
+    sibling = me + 1 - 2 * lax.rem(me, 2)
+    for k in range(n // 2):
         copy = remote(
             small.at[pl.ds(mine, PIECE), :], small_send.at[k], small_recv.at[k],
-            lax.rem(me + k, n),
+            sibling if k == 0 else lax.rem(me + 2 * k, n),
         )
         copy.start()
         small_copies.append(copy)
-    sibling = me + 1 - 2 * lax.rem(me, 2)
     big_copies = []
     for k in range(n // 2):
         copy = remote(
@@ -392,12 +392,25 @@
         axis=1,
     ).astype(f32)
 
-    for copy in small_copies:
+    chosen = [selection(q) for q in range(QUARTERS)]
+    for k in range(1, n // 2):
+        small_copies[k].wait_recv()
+        origin = pl.multiple_of(lax.rem(me + n - 2 * k, n) * PIECE, PIECE)
+        copy = remote(
+            small.at[pl.ds(origin, PIECE), :],
+            small_send.at[n // 2 + k],
+            small_recv.at[n // 2 + k],
+            sibling,
+        )
+        copy.start()
+        small_copies.append(copy)
+    small_copies[0].wait_recv()
+    for copy in small_copies[n // 2 :]:
         copy.wait_recv()
 
     parts = jnp.concatenate(thirds(small[...]), axis=1)
     for q in range(QUARTERS):
-        taken = nn(parts, selection(q))
+        taken = nn(parts, chosen[q])
         rows = slice(q * rows_q, (q + 1) * rows_q)
         left_emb[rows, :] = taken[:, 0:128].astype(bf16)
         right_emb[rows, :] = taken[:, 128:256].astype(bf16)
@@ -422,7 +435,7 @@
             hidden[rows, lanes] = gated.astype(bf16)
         return carry
 
-    lax.fori_loop(0, QUARTERS, front_step, 0)
+    lax.fori_loop(0, QUARTERS, front_step, 0, unroll=True)
 
     def first_step(q, carry):
         rows = chunk(q)
@@ -439,7 +452,7 @@
         diffused[rows, :] = result.astype(bf16)
         return carry
 
-    lax.fori_loop(0, QUARTERS, first_step, 0)
+    lax.fori_loop(0, QUARTERS, first_step, 0, unroll=True)
 
     pass_copies = []
     for k in range(1, n // 2):
@@ -458,7 +471,7 @@
         second[rows, :] = result.astype(bf16)
         return carry
 
-    lax.fori_loop(0, QUARTERS, second_step, 0)
+    lax.fori_loop(0, QUARTERS, second_step, 0, unroll=True)
 
     big_copies[0].wait_recv()
     for copy in pass_copies:
@@ -474,7 +487,7 @@
             twice[rows, lanes] = both[:, 128:]
         return carry
 
-    lax.fori_loop(0, QUARTERS, channel_step, 0)
+    lax.fori_loop(0, QUARTERS, channel_step, 0, unroll=True)
 
     def adjoint_step(q, carry):
         rows = chunk(q)
@@ -487,7 +500,7 @@
         stats[rows, 2:3] = jnp.sum(delta, axis=1, keepdims=True)
         return carry
 
-    lax.fori_loop(0, QUARTERS, adjoint_step, 0)
+    lax.fori_loop(0, QUARTERS, adjoint_step, 0, unroll=True)
 
     for copy in small_copies + big_copies + pass_copies:
         copy.wait_send()

time: 24.7 us -> 22.3 us (0.903)
  the two profiles are of different devices: /device:TPU:13 before, /device:TPU:4 now
where the time goes in v3:
time: 22.3 us; the launch traced here: 22.1 us
  Pallas kernels  20.9 us (94%)
  between operations  1.29 us (6%)
    pallas_call x1, Pallas kernels, whole_in_kernel(): pl.pallas_call(lambda *refs: gather_kernel(n, *refs), out_shape=(jax.Shap...  18.4 us
    pallas_call x1, Pallas kernels, whole_in_kernel(): pl.pallas_call(lambda *refs: finish_kernel(n, *refs), out_shape=outs, in_...  2.42 us

profile of v3, /device:TPU:4, one launch (start us, length us, event | category | flops | bytes accessed | tf_op | source)
XLA Modules:
  0.0 22.1 jit_solution(10330697902153850931)
XLA Ops:
  1.3 18.4 %shard_map.120 = (bf16[3,256,384]{2,1,0:T(8,128)(2,1)S(1)}, bf16[768,128]{1,0:T(8,128)(2,1)S(1)}, bf16[768,128]{1,0:T(8,128)(2,1)S(1)}, bf16[768,384]{1,0:T(8,12...) custom-call(s32[1]{0:T(128)S(6)} %copy.13.refs_0_, ...), custom_call_target="tpu_custom_call" | custom-call | tf_op jit(solution)/shard_map/pallas_call | solution.py:602
  19.7 2.4 %shard_map.121 = (bf16[48,384]{1,0:T(8,128)(2,1)}, f32[10,48]{1,0:T(8,128)}, f32[10,48]{1,0:T(8,128)}, f32[32,96]{1,0:T(8,128)}) custom-call(bf16[3,256,384]{2,1,0:T(8,128)(2,1)S(1)} %get-tuple-element.19.refs_0_, bf16[768,128]{1,0:T(8,128)(2,1)S(1)} %get-tuple-element.20.refs_1_, bf16[768,128]{1,0:T(8,128)(2,1)S(1)} %get-tuple-element.21.refs_2_, ...), custom_call_target="tpu_custom_call" | custom-call | tf_op jit(solution)/shard_map/pallas_call | solution.py:640

commit v4 on v3

--- a/solution.py
+++ b/solution.py
@@ -308,7 +308,7 @@
             ]
         )
     ]
-    for load in loads:
+    for load in loads[:4]:
         load.start()
     me = lax.axis_index("sensor")
     rows_q = PIECE * n
@@ -319,6 +319,8 @@
             barrier, inc=1, device_id={"sensor": lax.rem(me + k, n)},
             device_id_type=pl.DeviceIdType.MESH,
         )
+    for load in loads[4:]:
+        load.start()
     mine = pl.multiple_of(me * PIECE, PIECE)
 
     wanted = ones_where(iota((16, series.shape[1]), 1) == iota((16, series.shape[1]), 0) + starts[0])

time: 22.3 us -> 22.3 us (level)
  the two profiles are of different devices: /device:TPU:4 before, /device:TPU:6 now
where the time goes in v4:
time: 22.3 us; the launch traced here: 22.1 us
  Pallas kernels  20.9 us (94%)
  between operations  1.29 us (6%)
    pallas_call x1, Pallas kernels, whole_in_kernel(): pl.pallas_call(lambda *refs: gather_kernel(n, *refs), out_shape=(jax.Shap...  18.4 us
    pallas_call x1, Pallas kernels, whole_in_kernel(): pl.pallas_call(lambda *refs: finish_kernel(n, *refs), out_shape=outs, in_...  2.42 us

profile of v4, /device:TPU:6, one launch (start us, length us, event | category | flops | bytes accessed | tf_op | source)
XLA Modules:
  0.0 22.1 jit_solution(1587537609331264529)
XLA Ops:
  1.3 18.4 %shard_map.120 = (bf16[3,256,384]{2,1,0:T(8,128)(2,1)S(1)}, bf16[768,128]{1,0:T(8,128)(2,1)S(1)}, bf16[768,128]{1,0:T(8,128)(2,1)S(1)}, bf16[768,384]{1,0:T(8,12...) custom-call(s32[1]{0:T(128)S(6)} %copy.13.refs_0_, ...), custom_call_target="tpu_custom_call" | custom-call | tf_op jit(solution)/shard_map/pallas_call | solution.py:604
  19.7 2.4 %shard_map.121 = (bf16[48,384]{1,0:T(8,128)(2,1)}, f32[10,48]{1,0:T(8,128)}, f32[10,48]{1,0:T(8,128)}, f32[32,96]{1,0:T(8,128)}) custom-call(bf16[3,256,384]{2,1,0:T(8,128)(2,1)S(1)} %get-tuple-element.19.refs_0_, bf16[768,128]{1,0:T(8,128)(2,1)S(1)} %get-tuple-element.20.refs_1_, bf16[768,128]{1,0:T(8,128)(2,1)S(1)} %get-tuple-element.21.refs_2_, ...), custom_call_target="tpu_custom_call" | custom-call | tf_op jit(solution)/shard_map/pallas_call | solution.py:642
